TPU v7x, 256 devices: a whole 4x4x8 slice. The times are simulated.
256 devices in a mesh: row: 8 (over x, core), col: 32 (over z, y).
Axes of the slice: x: 4, y: 4, z: 8, core: 2. Of those that a mesh axis runs over, the one named last changes fastest.
Arguments:
- source_pcs: bfloat16 [32768, 64], P('row'), may hold values from -8 to 8
- target_pcs: bfloat16 [131072, 64], P('col'), may hold values from -8 to 8
- source_mass: float32 [32768], P('row'), may hold values from 0.25 to 4
- target_mass: float32 [131072], P('col'), may hold values from 0.25 to 4
- source_scaling: float32 [32768], P('row'), may hold values from 0.1 to 10
- labels: int32 [131072], P('col'), may hold values from 0 to 31
Outputs:
- fates: float32 [32768, 32], P(('row', 'col'))
- source_potential: float32 [32768], P(('row', 'col'))
- target_potential: float32 [131072], P('col')
All inputs are finite; a program needn't handle non-finite values.
Results may differ from a plain program's by a relative error of at most 0.00035.
Values may be sent and summed in bfloat16 or wider, within the bound.
No kernel may reach another device: no remote copies, remote signals or barrier semaphores. Data moves between devices by JAX's collectives and lax.ppermute only.
A program may use at most 128 MiB of HBM per device.

v0:
```python
import jax
import jax.numpy as jnp
from jax import lax
from jax.sharding import PartitionSpec as P

SETS = 32
ITERS = 2
entropy_weight = 0.5
offset_small = 1e-06


def kernel_rows(source_pcs, source_sq, target_pcs, target_sq, inverse, first_row, row_count):
    source_block = lax.dynamic_slice_in_dim(source_pcs, first_row, row_count, 0)
    block_sq = lax.dynamic_slice_in_dim(source_sq, first_row, row_count, 0)
    inner_products = lax.dot_general(
        source_block, target_pcs, (((1,), (1,)), ((), ())), preferred_element_type=jnp.float32
    )
    exponent = (block_sq[:, None] + target_sq[None, :] - 2.0 * inner_products) * inverse
    return jnp.exp(-exponent).astype(jnp.bfloat16)


def on_device(source_pcs, target_pcs, source_mass, target_mass, source_scaling, labels):
    row_count = source_pcs.shape[0]
    col_count = target_pcs.shape[0]
    source_wide = source_pcs.astype(jnp.float32)
    target_wide = target_pcs.astype(jnp.float32)
    source_sq = jnp.sum(source_wide * source_wide, 1)
    target_sq = jnp.sum(target_wide * target_wide, 1)
    source_sum, source_sqsum = lax.psum((jnp.sum(source_wide, 0), jnp.sum(source_sq)), "row")
    target_sum, target_sqsum = lax.psum((jnp.sum(target_wide, 0), jnp.sum(target_sq)), "col")
    source_total = row_count * lax.axis_size("row")
    target_total = col_count * lax.axis_size("col")
    mean_square = (
        source_sqsum / source_total
        + target_sqsum / target_total
        - 2.0 * jnp.sum(source_sum / source_total * (target_sum / target_total))
        + offset_small
    )
    inverse = 1.0 / (entropy_weight * mean_square)
    block_rows = min(row_count, 512)
    block_count = row_count // block_rows

    def one_block(block_index):
        return kernel_rows(
            source_pcs,
            source_sq,
            target_pcs,
            target_sq,
            inverse,
            block_index * block_rows,
            block_rows,
        )

    kernel = lax.map(one_block, jnp.arange(block_count, dtype=jnp.int32)).reshape(
        row_count, col_count
    )

    def row_pass(right_side):
        return jnp.dot(kernel, right_side, preferred_element_type=jnp.float32)

    share_rows = row_count // lax.axis_size("col")
    own_first = lax.axis_index("col") * share_rows
    own_mass = lax.dynamic_slice_in_dim(source_mass, own_first, share_rows, 0)
    scaled = source_scaling.astype(jnp.bfloat16)
    target_scaling = target_mass
    for iteration in range(ITERS):
        column_sums = lax.psum(jnp.dot(scaled, kernel, preferred_element_type=jnp.float32), "row")
        target_scaling = target_mass / column_sums
        if iteration + 1 < ITERS:
            update_right_side = target_scaling.astype(jnp.bfloat16)
            row_sums = lax.psum(row_pass(update_right_side), "col")
            scaled = (source_mass / row_sums).astype(jnp.bfloat16)
    membership = labels[:, None] == jnp.arange(SETS, dtype=jnp.int32)[None, :]
    probes = jnp.where(
        membership, target_scaling.astype(jnp.bfloat16)[:, None], jnp.zeros((), jnp.bfloat16)
    )
    all_sums = lax.psum(row_pass(probes), "col")
    own_sums = lax.dynamic_slice_in_dim(all_sums, own_first, share_rows, 0)
    totals = jnp.sum(own_sums, 1)
    fates = own_sums / totals[:, None]
    source_potential = entropy_weight * jnp.log(own_mass / totals)
    target_potential = entropy_weight * jnp.log(target_scaling)
    return (fates, source_potential, target_potential)


def solution(mesh):
    placed = (P("row", None), P("col", None), P("row"), P("col"), P("row"), P("col"))
    return jax.shard_map(
        on_device,
        mesh=mesh,
        in_specs=placed,
        out_specs=(P(("row", "col"), None), P(("row", "col")), P("col")),
        check_vma=False,
    )
```

profile of v0, /device:TPU:2, one launch (start us, length us, event | category | flops | bytes accessed | tf_op | source)
XLA Modules:
  0.0 551.6 jit_solution(15440935241534829660)
XLA Ops:
  7.2 0.0 all-reduce.4.cloned.1.call-start
  7.2 2.2 convert_reduce_fusion
  9.5 12.3 %all-reduce.1 = (f32[]{:T(128)}, f32[64]{0:T(128)S(1)}) all-reduce(f32[]{:T(128)} %get-tuple-element.75, f32[64]{0:T(128)S(1)} %get-tuple-element.76), channel_id=1, replica_groups=mesh['row'=8,'col'=32] {'row'}, use_global_device_ids=true, to_apply=%region_3.0 | all-reduce | flops 65 | bytes 520 | tf_op jit(solution)/shard_map/psum | solution.py:29
  22.4 78.6 %all-reduce = (f32[]{:T(128)}, f32[64]{0:T(128)S(1)}) all-reduce(f32[]{:T(128)} %get-tuple-element.50, f32[64]{0:T(128)S(1)} %get-tuple-element.49), channel_id=1, replica_groups=mesh['row'=8,'col'=32] {'col'}, use_global_device_ids=true, to_apply=%region_5.0 | all-reduce | flops 65 | bytes 520 | tf_op jit(solution)/shard_map/psum | solution.py:30
  101.6 0.6 multiply_reduce_fusion
  102.9 0.0 copy-start.3
  102.9 52.0 %while.10 = (s32[]{:T(128)}, bf16[8,512,4096]{2,1,0:T(8,128)(2,1)}, s32[8]{0:T(128)S(1)}, f32[4096]{0:T(1024)S(1)}, f32[4096]{0:T(1024)S(1)}, /*index=5*/bf16[40...) while((s32[]{:T(128)}, bf16[8,512,4096]{2,1,0:T(8,128)(2,1)}, ...), condition=%wide.region_12.13_spmd, body=%wide.region_11.12_spmd.sunk | while | flops 281018368 | bytes 4807863 | solution.py:54
  103.0 0.6 dynamic_slice.29
  104.2 0.1 dynamic_slice.30
  104.3 5.2 fusion.31
  109.4 0.6 dynamic_slice.29
  110.7 0.1 dynamic_slice.30
  110.7 5.2 fusion.31
  116.0 0.6 dynamic_slice.29
  117.2 0.1 dynamic_slice.30
  117.3 5.2 fusion.31
  122.5 0.6 dynamic_slice.29
  123.7 0.1 dynamic_slice.30
  123.8 5.2 fusion.31
  129.0 0.6 dynamic_slice.29
  130.2 0.1 dynamic_slice.30
  130.3 5.2 fusion.31
  135.5 0.6 dynamic_slice.29
  136.7 0.1 dynamic_slice.30
  136.8 5.2 fusion.31
  142.0 0.6 dynamic_slice.29
  143.2 0.1 dynamic_slice.30
  143.3 5.2 fusion.31
  148.5 0.6 dynamic_slice.29
  149.7 0.1 dynamic_slice.30
  149.8 5.2 fusion.31
  155.0 0.0 copy-done.3
  155.0 0.0 copy-start
  155.0 0.0 copy-start.1
  155.0 12.8 %fusion.15 = f32[1,4096]{1,0:T(1,128)S(1)} fusion(bf16[4096,4096]{1,0:T(8,128)(2,1)} %bitcast.23, bf16[4096,1]{0,1:T(2,128)(2,1)S(1)} %reshape.17), kind=kOutput, calls=%fused_computation.29 | convolution fusion | flops 33554432 | bytes 33579008 | tf_op jit(solution)/shard_map/dot_general | solution.py:67
  167.8 23.6 %psum.60 = f32[4096]{0:T(1024)S(1)} all-reduce(f32[4096]{0:T(1024)S(1)} %bitcast.28), channel_id=1, replica_groups=mesh['row'=8,'col'=32] {'row'}, use_global_device_ids=true, to_apply=%region_13.14 | all-reduce | flops 4096 | bytes 32768 | tf_op jit(solution)/shard_map/psum | solution.py:67
  191.5 0.0 copy-done
  191.5 0.0 copy-start.2
  191.5 15.0 %fusion.16 = f32[1,4096]{1,0:T(1,128)S(1)} fusion(bf16[4096,4096]{1,0:T(8,128)(2,1)} %bitcast.24, bf16[4096,1]{0,1:T(2,128)(2,1)S(1)} %reshape.19), kind=kOutput, calls=%fused_computation.30 | convolution fusion | flops 33554432 | bytes 33579008 | tf_op jit(solution)/shard_map/dot_general | solution.py:59
  206.5 137.7 %psum.61 = f32[4096]{0:T(1024)S(1)} all-reduce(f32[4096]{0:T(1024)S(1)} %bitcast.27), channel_id=1, replica_groups=mesh['row'=8,'col'=32] {'col'}, use_global_device_ids=true, to_apply=%region_14.15 | all-reduce | flops 4096 | bytes 32768 | tf_op jit(solution)/shard_map/psum | solution.py:71
  344.2 0.0 copy-done.1
  344.2 12.8 %fusion.17 = f32[1,4096]{1,0:T(1,128)S(1)} fusion(bf16[4096,1]{0,1:T(2,128)(2,1)S(1)} %reshape.21, bf16[4096,4096]{1,0:T(8,128)(2,1)} %bitcast.25), kind=kOutput, calls=%fused_computation.31 | convolution fusion | flops 33554432 | bytes 33579008 | tf_op jit(solution)/shard_map/dot_general | solution.py:67
  357.0 23.7 %psum.62 = f32[4096]{0:T(1024)S(1)} all-reduce(f32[4096]{0:T(1024)S(1)} %bitcast.29), channel_id=1, replica_groups=mesh['row'=8,'col'=32] {'row'}, use_global_device_ids=true, to_apply=%region_15.16 | all-reduce | flops 4096 | bytes 32768 | tf_op jit(solution)/shard_map/psum | solution.py:67
  380.7 0.6 log_multiply_fusion
  381.4 0.0 copy-done.2
  381.4 16.6 %fusion.9 = f32[4096,32]{0,1:T(8,128)} fusion(bf16[4096,4096]{1,0:T(8,128)(2,1)} %bitcast.26, s32[4096]{0:T(1024)S(1)} %copy-done.2, bf16[4096]{0:T(1024)(128)(2,1)S(1)} %get-tuple-element.73), kind=kOutput, calls=%fused_computation.15 | convolution fusion | flops 1074003968 | bytes 34103296 | tf_op jit(solution)/shard_map/dot_general | solution.py:59
  398.0 0.0 all-reduce.4.cloned.1.call-update
  398.0 144.0 %all-reduce.4.cloned.1.call-done = f32[4096,32]{0,1:T(8,128)} async-done(((f32[4096,32]{0,1:T(8,128)}), f32[4096,32]{0,1:T(8,128)}) %all-reduce.4.cloned.1.call-update) | async-done | bytes 524304 | tf_op jit(solution)/shard_map/psum | solution.py:77
  542.1 0.7 dynamic-slice_reduce_fusion
  542.8 0.6 log_multiply_fusion.1
  543.4 1.3 dynamic-slice_divide_fusion
  (8 shorter events, 0.1 us)
Async XLA Ops:
  7.2 534.9 %all-reduce.4.cloned.1.call-start = ((), (), s32[]{:S(2)}) async-start(), calls=%async_computation | async-start | bytes 1048576 | tf_op jit(solution)/shard_map/psum | solution.py:77
  102.9 52.0 %copy-start.3 = (f32[4096]{0:T(1024)S(1)}, f32[4096]{0:T(1024)}, u32[]{:S(2)}) copy-start(f32[4096]{0:T(1024)} %param.12) | copy-start | bytes 49156
  155.0 36.5 %copy-start = (f32[4096]{0:T(1024)S(1)}, f32[4096]{0:T(1024)}, u32[]{:S(2)}) copy-start(f32[4096]{0:T(1024)} %param.11) | copy-start | bytes 49156
  155.0 189.2 %copy-start.1 = (f32[4096]{0:T(1024)S(1)}, f32[4096]{0:T(1024)}, u32[]{:S(2)}) copy-start(f32[4096]{0:T(1024)} %param.10) | copy-start | bytes 49156
  191.5 189.9 %copy-start.2 = (s32[4096]{0:T(1024)S(1)}, s32[4096]{0:T(1024)}, u32[]{:S(2)}) copy-start(s32[4096]{0:T(1024)} %param.13) | copy-start | bytes 49156
Sparse Core Ops, SparseCore 0:
  398.2 143.8 all-reduce.3
where the time goes:
time: 552 us
  blocking collectives  276 us (50%)
  waiting for transfers between devices  144 us (26%)
  matrix products  98.7 us (18%)
  between operations  16.1 us (3%)
  other arithmetic  6.15 us (1%)
    psum x1, waiting for transfers between devices, on_device(): all_sums = lax.psum(row_pass(probes), 'col')  144 us
    psum x1, blocking collectives, on_device(): row_sums = lax.psum(row_pass(update_right_side), 'col')  138 us
    psum x1, blocking collectives, on_device(): lax.psum((jnp.sum(target_wide, 0), jnp.sum(target_sq)), 'col')  78.6 us
    psum x2, blocking collectives, on_device(): lax.psum(jnp.dot(scaled, kernel, preferred_element_type=jnp.float32), 'row')  47.3 us
    dot_general x8, matrix products, kernel_rows(): lax.dot_general(source_block, target_pcs, (((1,), (1,)), ((), ())), prefe...  41.5 us
    dot_general x2, matrix products, row_pass(): return jnp.dot(kernel, right_side, preferred_element_type=jnp.float32)  31.6 us
    dot_general x2, matrix products, on_device(): jnp.dot(scaled, kernel, preferred_element_type=jnp.float32)  25.7 us
    psum x1, blocking collectives, on_device(): lax.psum((jnp.sum(source_wide, 0), jnp.sum(source_sq)), 'row')  12.3 us
  transfers between devices with their start and end apart: 1, of which 1 were waited for; matrix products, arithmetic and copies ran while one was open for 0% of the time, Pallas kernels for 0%

commit v1 on v0

--- a/solution.py
+++ b/solution.py
@@ -68,7 +68,8 @@
         target_scaling = target_mass / column_sums
         if iteration + 1 < ITERS:
             update_right_side = target_scaling.astype(jnp.bfloat16)
-            row_sums = lax.psum(row_pass(update_right_side), "col")
+            state = row_pass(update_right_side)
+            row_sums = jnp.sum(lax.all_gather(state, axis_name="col"), axis=0)
             scaled = (source_mass / row_sums).astype(jnp.bfloat16)
     membership = labels[:, None] == jnp.arange(SETS, dtype=jnp.int32)[None, :]
     probes = jnp.where(

time: 552 us -> 464 us (0.84)
  blocking collectives: 276 us -> 185 us
    psum x1 -> x0, blocking collectives: 138 us -> none  [on_device(): row_sums = lax.psum(row_pass(update_right_side), 'col')]
    all_gather x0 -> x1, blocking collectives: none -> 46.3 us  [on_device(): row_sums = jnp.sum(lax.all_gather(state, axis_name='col'), axis=0)]
where the time goes in v1:
time: 464 us; the launch traced here: 463 us
  blocking collectives  185 us (40%)
  waiting for transfers between devices  147 us (32%)
  matrix products  98.7 us (21%)
  between operations  16.1 us (3%)
  other arithmetic  6.2 us (1%)
  local copies, waits for them, and re-layouts  5.44 us (1%)
  loops' own time  5.28 us (1%)
    psum x1, waiting for transfers between devices, on_device(): all_sums = lax.psum(row_pass(probes), 'col')  147 us
    psum x1, blocking collectives, on_device(): lax.psum((jnp.sum(target_wide, 0), jnp.sum(target_sq)), 'col')  78.6 us
    psum x2, blocking collectives, on_device(): lax.psum(jnp.dot(scaled, kernel, preferred_element_type=jnp.float32), 'row')  47.4 us
    all_gather x1, blocking collectives, on_device(): row_sums = jnp.sum(lax.all_gather(state, axis_name='col'), axis=0)  46.3 us
    dot_general x8, matrix products, kernel_rows(): lax.dot_general(source_block, target_pcs, (((1,), (1,)), ((), ())), prefe...  41.5 us
    dot_general x2, matrix products, row_pass(): return jnp.dot(kernel, right_side, preferred_element_type=jnp.float32)  31.6 us
    dot_general x2, matrix products, on_device(): jnp.dot(scaled, kernel, preferred_element_type=jnp.float32)  25.7 us
    psum x1, blocking collectives, on_device(): lax.psum((jnp.sum(source_wide, 0), jnp.sum(source_sq)), 'row')  12.3 us
  transfers between devices with their start and end apart: 1, of which 1 were waited for; matrix products, arithmetic and copies ran while one was open for 0% of the time, Pallas kernels for 0%

profile of v1, /device:TPU:2, one launch (start us, length us, event | category | flops | bytes accessed | tf_op | source)
XLA Modules:
  0.0 463.0 jit_solution(607848139816923332)
XLA Ops:
  7.2 0.0 all-reduce.4.cloned.1.call-start
  7.2 2.2 convert_reduce_fusion
  9.5 12.3 %all-reduce.1 = (f32[]{:T(128)}, f32[64]{0:T(128)S(1)}) all-reduce(f32[]{:T(128)} %get-tuple-element.75, f32[64]{0:T(128)S(1)} %get-tuple-element.76), channel_id=1, replica_groups=mesh['row'=8,'col'=32] {'row'}, use_global_device_ids=true, to_apply=%region_3.0 | all-reduce | flops 65 | bytes 520 | tf_op jit(solution)/shard_map/psum | solution.py:29
  22.4 78.6 %all-reduce = (f32[]{:T(128)}, f32[64]{0:T(128)S(1)}) all-reduce(f32[]{:T(128)} %get-tuple-element.50, f32[64]{0:T(128)S(1)} %get-tuple-element.49), channel_id=1, replica_groups=mesh['row'=8,'col'=32] {'col'}, use_global_device_ids=true, to_apply=%region_5.0 | all-reduce | flops 65 | bytes 520 | tf_op jit(solution)/shard_map/psum | solution.py:30
  101.6 0.6 multiply_reduce_fusion
  102.9 0.0 copy-start.3
  102.9 52.0 %while.10 = (s32[]{:T(128)}, bf16[8,512,4096]{2,1,0:T(8,128)(2,1)}, s32[8]{0:T(128)S(1)}, f32[4096]{0:T(1024)S(1)}, f32[4096]{0:T(1024)S(1)}, /*index=5*/bf16[40...) while((s32[]{:T(128)}, bf16[8,512,4096]{2,1,0:T(8,128)(2,1)}, ...), condition=%wide.region_12.13_spmd, body=%wide.region_11.12_spmd.sunk | while | flops 281018368 | bytes 4807863 | solution.py:54
  103.0 0.6 dynamic_slice.29
  104.2 0.1 dynamic_slice.30
  104.3 5.2 %fusion.31 = bf16[8,512,4096]{2,1,0:T(8,128)(2,1)} fusion(bf16[8,512,4096]{2,1,0:T(8,128)(2,1)} %get-tuple-element.139, s32[]{:T(128)} %get-tuple-element.138, bf16[4096,64]{0,1:T(8,128)(2,1)} %get-tuple-element.156, f32[]{:T(128)} %get-tuple-element.157, f32[4096]{0:T(1024)S(1)} %get-tuple-element.154, f32[512]{0:T(512)S(1)} %dynamic_slice.30, ...), kind=kOutput, calls=%fused_computation.2.clone.1 | convolution fusion | flops 281018368 | bytes 4803588 | tf_op jit(solution)/shard_map/while/body/eval_jaxpr/dot_general | solution.py:15
  109.4 0.6 dynamic_slice.29
  110.7 0.1 dynamic_slice.30
  110.7 5.2 %fusion.31 = bf16[8,512,4096]{2,1,0:T(8,128)(2,1)} fusion(bf16[8,512,4096]{2,1,0:T(8,128)(2,1)} %get-tuple-element.139, s32[]{:T(128)} %get-tuple-element.138, bf16[4096,64]{0,1:T(8,128)(2,1)} %get-tuple-element.156, f32[]{:T(128)} %get-tuple-element.157, f32[4096]{0:T(1024)S(1)} %get-tuple-element.154, f32[512]{0:T(512)S(1)} %dynamic_slice.30, ...), kind=kOutput, calls=%fused_computation.2.clone.1 | convolution fusion | flops 281018368 | bytes 4803588 | tf_op jit(solution)/shard_map/while/body/eval_jaxpr/dot_general | solution.py:15
  116.0 0.6 dynamic_slice.29
  117.2 0.1 dynamic_slice.30
  117.3 5.2 %fusion.31 = bf16[8,512,4096]{2,1,0:T(8,128)(2,1)} fusion(bf16[8,512,4096]{2,1,0:T(8,128)(2,1)} %get-tuple-element.139, s32[]{:T(128)} %get-tuple-element.138, bf16[4096,64]{0,1:T(8,128)(2,1)} %get-tuple-element.156, f32[]{:T(128)} %get-tuple-element.157, f32[4096]{0:T(1024)S(1)} %get-tuple-element.154, f32[512]{0:T(512)S(1)} %dynamic_slice.30, ...), kind=kOutput, calls=%fused_computation.2.clone.1 | convolution fusion | flops 281018368 | bytes 4803588 | tf_op jit(solution)/shard_map/while/body/eval_jaxpr/dot_general | solution.py:15
  122.5 0.6 dynamic_slice.29
  123.7 0.1 dynamic_slice.30
  123.8 5.2 %fusion.31 = bf16[8,512,4096]{2,1,0:T(8,128)(2,1)} fusion(bf16[8,512,4096]{2,1,0:T(8,128)(2,1)} %get-tuple-element.139, s32[]{:T(128)} %get-tuple-element.138, bf16[4096,64]{0,1:T(8,128)(2,1)} %get-tuple-element.156, f32[]{:T(128)} %get-tuple-element.157, f32[4096]{0:T(1024)S(1)} %get-tuple-element.154, f32[512]{0:T(512)S(1)} %dynamic_slice.30, ...), kind=kOutput, calls=%fused_computation.2.clone.1 | convolution fusion | flops 281018368 | bytes 4803588 | tf_op jit(solution)/shard_map/while/body/eval_jaxpr/dot_general | solution.py:15
  129.0 0.6 dynamic_slice.29
  130.2 0.1 dynamic_slice.30
  130.3 5.2 %fusion.31 = bf16[8,512,4096]{2,1,0:T(8,128)(2,1)} fusion(bf16[8,512,4096]{2,1,0:T(8,128)(2,1)} %get-tuple-element.139, s32[]{:T(128)} %get-tuple-element.138, bf16[4096,64]{0,1:T(8,128)(2,1)} %get-tuple-element.156, f32[]{:T(128)} %get-tuple-element.157, f32[4096]{0:T(1024)S(1)} %get-tuple-element.154, f32[512]{0:T(512)S(1)} %dynamic_slice.30, ...), kind=kOutput, calls=%fused_computation.2.clone.1 | convolution fusion | flops 281018368 | bytes 4803588 | tf_op jit(solution)/shard_map/while/body/eval_jaxpr/dot_general | solution.py:15
  135.5 0.6 dynamic_slice.29
  136.7 0.1 dynamic_slice.30
  136.8 5.2 %fusion.31 = bf16[8,512,4096]{2,1,0:T(8,128)(2,1)} fusion(bf16[8,512,4096]{2,1,0:T(8,128)(2,1)} %get-tuple-element.139, s32[]{:T(128)} %get-tuple-element.138, bf16[4096,64]{0,1:T(8,128)(2,1)} %get-tuple-element.156, f32[]{:T(128)} %get-tuple-element.157, f32[4096]{0:T(1024)S(1)} %get-tuple-element.154, f32[512]{0:T(512)S(1)} %dynamic_slice.30, ...), kind=kOutput, calls=%fused_computation.2.clone.1 | convolution fusion | flops 281018368 | bytes 4803588 | tf_op jit(solution)/shard_map/while/body/eval_jaxpr/dot_general | solution.py:15
  142.0 0.6 dynamic_slice.29
  143.2 0.1 dynamic_slice.30
  143.3 5.2 %fusion.31 = bf16[8,512,4096]{2,1,0:T(8,128)(2,1)} fusion(bf16[8,512,4096]{2,1,0:T(8,128)(2,1)} %get-tuple-element.139, s32[]{:T(128)} %get-tuple-element.138, bf16[4096,64]{0,1:T(8,128)(2,1)} %get-tuple-element.156, f32[]{:T(128)} %get-tuple-element.157, f32[4096]{0:T(1024)S(1)} %get-tuple-element.154, f32[512]{0:T(512)S(1)} %dynamic_slice.30, ...), kind=kOutput, calls=%fused_computation.2.clone.1 | convolution fusion | flops 281018368 | bytes 4803588 | tf_op jit(solution)/shard_map/while/body/eval_jaxpr/dot_general | solution.py:15
  148.5 0.6 dynamic_slice.29
  149.7 0.1 dynamic_slice.30
  149.8 5.2 %fusion.31 = bf16[8,512,4096]{2,1,0:T(8,128)(2,1)} fusion(bf16[8,512,4096]{2,1,0:T(8,128)(2,1)} %get-tuple-element.139, s32[]{:T(128)} %get-tuple-element.138, bf16[4096,64]{0,1:T(8,128)(2,1)} %get-tuple-element.156, f32[]{:T(128)} %get-tuple-element.157, f32[4096]{0:T(1024)S(1)} %get-tuple-element.154, f32[512]{0:T(512)S(1)} %dynamic_slice.30, ...), kind=kOutput, calls=%fused_computation.2.clone.1 | convolution fusion | flops 281018368 | bytes 4803588 | tf_op jit(solution)/shard_map/while/body/eval_jaxpr/dot_general | solution.py:15
  155.0 0.0 copy-done.3
  155.0 0.0 copy-start
  155.0 0.0 copy-start.1
  155.0 12.8 %fusion.15 = f32[1,4096]{1,0:T(1,128)S(1)} fusion(bf16[4096,4096]{1,0:T(8,128)(2,1)} %bitcast.23, bf16[4096,1]{0,1:T(2,128)(2,1)S(1)} %reshape.18), kind=kOutput, calls=%fused_computation.29 | convolution fusion | flops 33554432 | bytes 33579008 | tf_op jit(solution)/shard_map/dot_general | solution.py:67
  167.8 23.6 %psum.53 = f32[4096]{0:T(1024)S(1)} all-reduce(f32[4096]{0:T(1024)S(1)} %bitcast.28), channel_id=1, replica_groups=mesh['row'=8,'col'=32] {'row'}, use_global_device_ids=true, to_apply=%region_13.14 | all-reduce | flops 4096 | bytes 32768 | tf_op jit(solution)/shard_map/psum | solution.py:67
  191.5 0.0 copy-done
  191.5 0.0 copy-start.2
  191.5 15.0 %fusion.16 = f32[1,4096]{1,0:T(1,128)S(1)} fusion(bf16[4096,4096]{1,0:T(8,128)(2,1)} %bitcast.24, bf16[4096,1]{0,1:T(2,128)(2,1)S(1)} %reshape.20), kind=kOutput, calls=%fused_computation.30 | convolution fusion | flops 33554432 | bytes 33579008 | tf_op jit(solution)/shard_map/dot_general | solution.py:59
  206.5 46.3 %all-gather = f32[131072]{0:T(1024)S(1)} all-gather(f32[4096]{0:T(1024)S(1)} %bitcast.27), channel_id=2, replica_groups=mesh['row'=8,'col'=32] {'col'}, dimensions={0}, use_global_device_ids=true | all-gather | bytes 540672 | tf_op jit(solution)/shard_map/all_gather | solution.py:72
  252.8 0.1 reshape.17
  252.9 0.1 reduce_sum.88
  253.0 0.0 copy-done.1
  253.0 12.8 %fusion.17 = f32[1,4096]{1,0:T(1,128)S(1)} fusion(bf16[4096,1]{0,1:T(2,128)(2,1)S(1)} %reshape.22, bf16[4096,4096]{1,0:T(8,128)(2,1)} %bitcast.25), kind=kOutput, calls=%fused_computation.31 | convolution fusion | flops 33554432 | bytes 33579008 | tf_op jit(solution)/shard_map/dot_general | solution.py:67
  265.8 23.8 %psum.54 = f32[4096]{0:T(1024)S(1)} all-reduce(f32[4096]{0:T(1024)S(1)} %bitcast.29), channel_id=1, replica_groups=mesh['row'=8,'col'=32] {'row'}, use_global_device_ids=true, to_apply=%region_15.16 | all-reduce | flops 4096 | bytes 32768 | tf_op jit(solution)/shard_map/psum | solution.py:67
  289.6 0.6 log_multiply_fusion
  290.2 0.0 copy-done.2
  290.2 16.6 %fusion.9 = f32[4096,32]{0,1:T(8,128)} fusion(bf16[4096,4096]{1,0:T(8,128)(2,1)} %bitcast.26, s32[4096]{0:T(1024)S(1)} %copy-done.2, bf16[4096]{0:T(1024)(128)(2,1)S(1)} %get-tuple-element.73), kind=kOutput, calls=%fused_computation.15 | convolution fusion | flops 1074003968 | bytes 34103296 | tf_op jit(solution)/shard_map/dot_general | solution.py:59
  306.9 0.0 all-reduce.4.cloned.1.call-update
  306.9 146.6 %all-reduce.4.cloned.1.call-done = f32[4096,32]{0,1:T(8,128)} async-done(((f32[4096,32]{0,1:T(8,128)}), f32[4096,32]{0,1:T(8,128)}) %all-reduce.4.cloned.1.call-update) | async-done | bytes 524304 | tf_op jit(solution)/shard_map/psum | solution.py:78
  453.5 0.7 dynamic-slice_reduce_fusion
  454.2 0.6 log_multiply_fusion.1
  454.8 1.3 dynamic-slice_divide_fusion
  (8 shorter events, 0.1 us)
Async XLA Ops:
  7.2 446.3 %all-reduce.4.cloned.1.call-start = ((), (), s32[]{:S(2)}) async-start(), calls=%async_computation | async-start | bytes 1048576 | tf_op jit(solution)/shard_map/psum | solution.py:78
  102.9 52.0 %copy-start.3 = (f32[4096]{0:T(1024)S(1)}, f32[4096]{0:T(1024)}, u32[]{:S(2)}) copy-start(f32[4096]{0:T(1024)} %param.12) | copy-start | bytes 49156
  155.0 36.5 %copy-start = (f32[4096]{0:T(1024)S(1)}, f32[4096]{0:T(1024)}, u32[]{:S(2)}) copy-start(f32[4096]{0:T(1024)} %param.11) | copy-start | bytes 49156
  155.0 98.0 %copy-start.1 = (f32[4096]{0:T(1024)S(1)}, f32[4096]{0:T(1024)}, u32[]{:S(2)}) copy-start(f32[4096]{0:T(1024)} %param.10) | copy-start | bytes 49156
  191.5 98.8 %copy-start.2 = (s32[4096]{0:T(1024)S(1)}, s32[4096]{0:T(1024)}, u32[]{:S(2)}) copy-start(s32[4096]{0:T(1024)} %param.13) | copy-start | bytes 49156
Sparse Core Ops, SparseCore 0:
  307.0 146.4 all-reduce.3
